TPU v7x, 32 devices: a whole 2x2x4 slice. The times are simulated.
32 devices in a mesh: sx: 4 (over z), sy: 4 (over y, x), dp: 2 (over core).
Axes of the slice: x: 2, y: 2, z: 4, core: 2. Of those that a mesh axis runs over, the one named last changes fastest.
Arguments:
- features: bfloat16 [2, 32, 32, 4, 8, 128], P('dp', 'sx', 'sy'), may hold values from -6 to 6
- cotangent: bfloat16 [2, 32, 32, 4, 8, 128], P('dp', 'sx', 'sy'), may hold values from -6 to 6
- first_weight: bfloat16 [27, 128, 128], replicated, may hold values from -0.109375 to 0.109375
- second_weight: bfloat16 [27, 128, 128], replicated, may hold values from -0.109375 to 0.109375
- neighbours: int32 [2, 4, 4, 4, 26], P('dp', 'sx', 'sy'), may hold values from -1 to 3, as said below
- counts: int32 [2, 4, 4], P('dp', 'sx', 'sy'), may hold values from 1 to 4, as said below
Outputs:
- out_field: bfloat16 [2, 32, 32, 4, 8, 128], P('dp', 'sx', 'sy')
- grad_input: bfloat16 [2, 32, 32, 4, 8, 128], P('dp', 'sx', 'sy')
- grad_first: float32 [27, 128, 128], replicated
- grad_second: float32 [27, 128, 128], replicated
Inputs may be any that keep to these rules, and one draw needn't show every extreme that they name: Entries name only live slots; slots at or above a column's count have no neighbours; the relation is symmetric: if slot s of column (i, j) names slot t in direction d, then slot t of column (i+dx, j+dy) names s in the opposite direction, and the blocks are adjacent in space; columns outside the grid are never named. `counts`: some column of every workpiece has 4 live slots.
All inputs are finite; a program needn't handle non-finite values.
Results may differ from a plain program's by a relative error of at most 0.012.
Values may be sent and summed in bfloat16 or wider, within the bound.
A program may use at most 192 MiB of HBM per device.

v0:
```python
import jax
import jax.numpy as jnp
from jax import lax
from jax.sharding import PartitionSpec as P


def with_halo(cells, sides, width):
    for axis, dim in sides:
        count = lax.axis_size(axis)
        ends = count - 1
        head = lax.slice_in_dim(cells, 0, width, axis=dim)
        tail = lax.slice_in_dim(cells, cells.shape[dim] - width, cells.shape[dim], axis=dim)
        cells = jnp.concatenate(
            [
                lax.ppermute(tail, axis, [(i, (i + 1) % count) for i in range(ends)]),
                cells,
                lax.ppermute(head, axis, [((i + 1) % count, i) for i in range(ends)]),
            ],
            axis=dim,
        )
    return cells


def padded_blocks(halo_field, neighbour):
    block_edge = halo_field.shape[0] - 2
    ranges_xy = [(0, 1), (1, block_edge + 1), (block_edge + 1, block_edge + 2)]
    ranges_z = [(block_edge - 1, block_edge), (0, block_edge), (0, 1)]
    planes = []
    for shift_x in range(3):
        row_list = []
        for shift_y in range(3):
            slab_list = []
            for shift_z in range(3):
                direction = shift_x * 9 + shift_y * 3 + shift_z
                low_x, high_x = ranges_xy[shift_x]
                low_y, high_y = ranges_xy[shift_y]
                low_z, high_z = ranges_z[shift_z]
                region = halo_field[low_x:high_x, low_y:high_y, :, low_z:high_z]
                if direction == 13:
                    slab_piece = region
                else:
                    entry = direction if direction < 13 else direction - 1
                    target = neighbour[:, entry]
                    valid = (target >= 0).astype(region.dtype)[None, None, :, None, None]
                    slab_piece = jnp.take(region, jnp.maximum(target, 0), axis=2) * valid
                slab_list.append(slab_piece)
            row_list.append(jnp.concatenate(slab_list, axis=3))
        planes.append(jnp.concatenate(row_list, axis=1))
    return jnp.concatenate(planes, axis=0)


def patch_matrix(padded, block_edge):
    pieces = []
    for shift_x in range(3):
        for shift_y in range(3):
            for shift_z in range(3):
                pieces.append(
                    padded[
                        shift_x : shift_x + block_edge,
                        shift_y : shift_y + block_edge,
                        :,
                        shift_z : shift_z + block_edge,
                    ]
                )
    stacked = jnp.concatenate(pieces, axis=-1)
    return stacked.reshape(-1, stacked.shape[-1])


def flipped_weight(weight):
    return jnp.transpose(weight[::-1], (0, 2, 1))


def silu_slope(values):
    logistic = jax.nn.sigmoid(values)
    return logistic * (1.0 + values * (1.0 - logistic))


def exchanged(values, neighbour):
    halo_field = with_halo(values, (("sx", 0), ("sy", 1)), 1)
    return patch_matrix(padded_blocks(halo_field, neighbour), values.shape[0])


def convolve(columns, weight, shape):
    matrix = weight.reshape(-1, weight.shape[2])
    return jnp.dot(columns, matrix, preferred_element_type=jnp.float32).reshape(shape)


def weight_partial(columns, grads):
    channels = grads.shape[-1]
    term = lax.dot_general(
        columns,
        grads.reshape(-1, channels),
        (((0,), (0,)), ((), ())),
        preferred_element_type=jnp.float32,
    )
    return term.reshape(27, channels, channels)


def sum_gradients(first_part, second_part):
    first_total, second_total = lax.psum((first_part, second_part), ("sx", "sy", "dp"))
    return (first_total, second_total)


def shards(features, cotangent, first_weight, second_weight, neighbours, counts):
    voxels_in = features[0]
    upstream = cotangent[0]
    neighbour = neighbours[0, 0, 0]
    block_edge = voxels_in.shape[0]
    slot_count = voxels_in.shape[2]
    shape = voxels_in.shape
    grad_scale = float(
        lax.axis_size("sx") * lax.axis_size("sy") * lax.axis_size("dp") * slot_count * block_edge**3
    ) ** (-0.5)
    live_mask = (jnp.arange(slot_count, dtype=jnp.int32) < counts[0, 0, 0]).astype(jnp.float32)[
        None, None, :, None, None
    ]
    masked = voxels_in * live_mask.astype(voxels_in.dtype)
    input_columns = exchanged(masked, neighbour)
    pre_first = convolve(input_columns, first_weight, shape)
    hidden = (jax.nn.silu(pre_first) * live_mask).astype(jnp.bfloat16)
    hidden_columns = exchanged(hidden, neighbour)
    pre_second = convolve(hidden_columns, second_weight, shape)
    summed = masked.astype(jnp.float32) + pre_second
    out_block = (jax.nn.silu(summed) * live_mask).astype(jnp.bfloat16)
    back_second = (upstream.astype(jnp.float32) * silu_slope(summed) * live_mask).astype(
        jnp.bfloat16
    )
    second_part = weight_partial(hidden_columns, back_second)
    back_hidden = convolve(exchanged(back_second, neighbour), flipped_weight(second_weight), shape)
    back_first = (back_hidden * silu_slope(pre_first) * live_mask).astype(jnp.bfloat16)
    first_part = weight_partial(input_columns, back_first)
    first_total, second_total = sum_gradients(first_part, second_part)
    back_input = convolve(exchanged(back_first, neighbour), flipped_weight(first_weight), shape)
    input_block = ((back_second.astype(jnp.float32) + back_input) * live_mask).astype(jnp.bfloat16)
    return (out_block[None], input_block[None], first_total * grad_scale, second_total * grad_scale)


def solution(mesh):
    in_specs = (
        P("dp", "sx", "sy", None, None, None),
        P("dp", "sx", "sy", None, None, None),
        P(),
        P(),
        P("dp", "sx", "sy", None, None),
        P("dp", "sx", "sy"),
    )
    out_specs = (
        P("dp", "sx", "sy", None, None, None),
        P("dp", "sx", "sy", None, None, None),
        P(),
        P(),
    )
    return jax.shard_map(shards, mesh=mesh, in_specs=in_specs, out_specs=out_specs, check_vma=False)
```

profile of v0, /device:TPU:0, one launch (start us, length us, event | category | flops | bytes accessed | tf_op | source)
XLA Modules:
  0.0 502.4 jit_solution(4962648479938337616)
XLA Ops:
  11.6 5.6 %collective-permute-start = (bf16[1,8,4,8,128]{4,3,2,1,0:T(8,128)(2,1)S(1)}, bf16[1,8,4,8,128]{4,3,2,1,0:T(8,128)(2,1)S(1)}, u32[]{:S(2)}, u32[]{:S(2)}) collective-permute-start(bf16[1,8,4,8,128]{4,3,2,1,0:T(8,128)(2,1)S(1)} %get-tuple-element.97), channel_id=1, source_target_pairs={{0,8},{8,16},{16,24},{1,9},{9,17},{17,25},{2,10},{10,18},{18,26},{... | collective-permute-start | bytes 196616 | tf_op jit(solution)/shard_map/ppermute | solution.py:15
  17.2 1.9 maximum_reduce_fusion.8
  19.1 2.4 fusion.137
  29.8 1.8 fusion.139
  58.4 4.7 collective-permute-start.2
  85.4 1.6 maximum_maximum_fusion.9
  87.0 2.2 maximum_maximum_fusion
  112.2 3.2 maximum_maximum_fusion.1
  124.6 8.5 %multiply_convert_fusion.1 = (bf16[8,8,4,8,128]{4,3,2,1,0:T(8,128)(2,1)S(1)}, f32[8,8,4,8,128]{4,3,2,1,0:T(8,128)}) fusion(f32[4]{0:T(128)S(1)} %copy-done.57, bf16[8,8,4,8,3456]{4,3,2,1,0:T(8,128)(2,1)} %slice_dynamic-update-slice_fusion.72, bf16[3456,128,1,1,1]{1,0,4,3,2:T(8,128)(2,1)S(1)} %bitcast.657), kind=kOutput, calls=%fused_computation.133 | convolution fusion | flops 1813512192 | bytes 16613392 | tf_op jit(solution)/shard_map/dot_general | solution.py:85
  134.6 4.6 collective-permute-start.4
  141.2 17.9 %copy.150 = bf16[3456,2048]{1,0:T(8,128)(2,1)} copy(bf16[3456,2048]{0,1:T(8,128)(2,1)} %bitcast.253) | data formatting | bytes 28311552 | tf_op jit(solution)/shard_map/dot_general | solution.py:90
  160.6 5.4 %collective-permute-start.6 = (bf16[10,1,4,8,128]{4,3,2,1,0:T(8,128)(2,1)S(1)}, bf16[10,1,4,8,128]{4,3,2,1,0:T(8,128)(2,1)S(1)}, u32[]{:S(2)}, u32[]{:S(2)}) collective-permute-start(bf16[10,1,4,8,128]{4,3,2,1,0:T(8,128)(2,1)S(1)} %get-tuple-element.79), channel_id=1, source_target_pairs={{0,2},{2,4},{4,6},{1,3},{3,5},{5,7},{8,10},{10,12},{12,14},{9,11},... | collective-permute-start | bytes 245768 | tf_op jit(solution)/shard_map/ppermute | solution.py:15
  180.5 2.0 maximum_maximum_fusion.11
  182.5 2.2 maximum_maximum_fusion.2
  207.4 3.2 maximum_maximum_fusion.3
  219.8 10.1 %fusion.6 = (bf16[8,8,4,8,128]{4,3,2,1,0:T(8,128)(2,1)S(1)}, bf16[1,8,8,4,8,128]{5,4,3,2,1,0:T(8,128)(2,1)}) fusion(bf16[1,8,8,4,8,128]{5,4,3,2,1,0:T(8,128)(2,1)S(1)} %copy-done.60, f32[4]{0:T(128)S(1)} %copy-done.57, bf16[8,8,4,8,3456]{4,3,2,1,0:T(8,128)(2,1)} %slice_dynamic-update-slice_fusion.48, bf16[3456,128,1,1,1]{1,0,4,3,2:T(8,128)(2,1)S(1)} %bitcast.658, ...), kind=kOutput, calls=%fused_computation.130 | convolution fusion | flops 1816133632 | bytes 17137680 | tf_op jit(solution)/shard_map/dot_general | solution.py:85
  231.6 4.5 collective-permute-start.8
  237.8 18.8 %copy.151 = bf16[3456,2048]{1,0:T(8,128)(2,1)} copy(bf16[3456,2048]{0,1:T(8,128)(2,1)} %bitcast.258) | data formatting | bytes 28311552 | tf_op jit(solution)/shard_map/dot_general | solution.py:90
  256.5 8.2 %fusion.180 = f32[27,128,128]{2,1,0:T(8,128)} fusion(bf16[27,128,2048]{2,1,0:T(8,128)(2,1)} %bitcast.651, bf16[2048,128,1]{1,0,2:T(8,128)(2,1)S(1)} %bitcast.648), kind=kOutput, calls=%fused_computation.762 | convolution fusion | flops 1811939328 | bytes 16449536 | tf_op jit(solution)/shard_map/dot_general | solution.py:90
  266.3 5.4 %collective-permute-start.10 = (bf16[10,1,4,8,128]{4,3,2,1,0:T(8,128)(2,1)S(1)}, bf16[10,1,4,8,128]{4,3,2,1,0:T(8,128)(2,1)S(1)}, u32[]{:S(2)}, u32[]{:S(2)}) collective-permute-start(bf16[10,1,4,8,128]{4,3,2,1,0:T(8,128)(2,1)S(1)} %get-tuple-element.77), channel_id=1, source_target_pairs={{0,2},{2,4},{4,6},{1,3},{3,5},{5,7},{8,10},{10,12},{12,14},{9,11},... | collective-permute-start | bytes 245768 | tf_op jit(solution)/shard_map/ppermute | solution.py:15
  287.7 2.2 maximum_maximum_fusion.4
  312.6 3.2 maximum_maximum_fusion.5
  325.0 9.1 %fusion.3 = bf16[8,8,4,8,128]{4,3,2,1,0:T(8,128)(2,1)S(1)} fusion(bf16[8,8,4,8,3456]{4,3,2,1,0:T(8,128)(2,1)} %slice_dynamic-update-slice_fusion.24, bf16[3456,128,1,1,1]{1,0,4,3,2:T(8,128)(2,1)S(1)} %bitcast.659, f32[8,8,4,8,128]{4,3,2,1,0:T(8,128)S(1)} %copy-done.61, f32[4]{0:T(128)S(1)} %copy-done.57), kind=kOutput, calls=%fused_computation.118 | convolution fusion | flops 1814560768 | bytes 16613392 | tf_op jit(solution)/shard_map/dot_general | solution.py:85
  335.6 4.8 collective-permute-start.12
  342.0 8.3 %fusion.179 = f32[27,128,128]{2,1,0:T(8,128)} fusion(bf16[27,128,2048]{2,1,0:T(8,128)(2,1)} %bitcast.650, bf16[2048,128,1]{1,0,2:T(8,128)(2,1)S(1)} %bitcast.649), kind=kOutput, calls=%fused_computation.761 | convolution fusion | flops 1811939328 | bytes 16449536 | tf_op jit(solution)/shard_map/dot_general | solution.py:90
  351.8 5.4 %collective-permute-start.14 = (bf16[10,1,4,8,128]{4,3,2,1,0:T(8,128)(2,1)S(1)}, bf16[10,1,4,8,128]{4,3,2,1,0:T(8,128)(2,1)S(1)}, u32[]{:S(2)}, u32[]{:S(2)}) collective-permute-start(bf16[10,1,4,8,128]{4,3,2,1,0:T(8,128)(2,1)S(1)} %get-tuple-element.75), channel_id=1, source_target_pairs={{0,2},{2,4},{4,6},{1,3},{3,5},{5,7},{8,10},{10,12},{12,14},{9,11},... | collective-permute-start | bytes 245768 | tf_op jit(solution)/shard_map/ppermute | solution.py:15
  371.6 1.6 maximum_maximum_fusion.15
  373.2 2.2 maximum_maximum_fusion.6
  398.1 3.2 maximum_maximum_fusion.7
  410.3 8.2 %fusion.4 = bf16[1,8,8,4,8,128]{5,4,3,2,1,0:T(8,128)(2,1)} fusion(bf16[8,8,4,8,3456]{4,3,2,1,0:T(8,128)(2,1)} %slice_dynamic-update-slice_fusion, bf16[3456,128,1,1,1]{1,0,4,3,2:T(8,128)(2,1)S(1)} %bitcast.656, bf16[8,8,4,8,128]{4,3,2,1,0:T(8,128)(2,1)S(1)} %get-tuple-element.65, f32[4]{0:T(128)S(1)} %copy-done.57), kind=kOutput, calls=%fused_computation.119 | convolution fusion | flops 1812987904 | bytes 16089104 | tf_op jit(solution)/shard_map/dot_general | solution.py:85
  418.6 72.3 %all-reduce.3.cloned.1.call-done = (f32[27,128,128]{2,1,0:T(8,128)}, f32[27,128,128]{2,1,0:T(8,128)}) async-done(((f32[27,128,128]{2,1,0:T(8,128)}, f32[27,128,128]{2,1,0:T(8,128)}), (f32[27,128,128]{2,1,0:T(8,128)}, f32[27,128,128]{2,1,0:T(8,128)})) %all-reduce.3.cloned.1.call-update) | async-done | bytes 3538960 | tf_op jit(solution)/shard_map/psum | solution.py:100
  490.9 3.0 broadcast_multiply_fusion.1
  (653 shorter events, 247.3 us)
Async XLA Ops:
  7.2 40.9 %copy-start.3 = (bf16[27,128,128]{2,1,0:T(8,128)(2,1)S(1)}, bf16[27,128,128]{2,1,0:T(8,128)(2,1)}, u32[]{:S(2)}) copy-start(bf16[27,128,128]{2,1,0:T(8,128)(2,1)} %param.23) | copy-start | bytes 2654212
  7.2 483.7 %all-reduce.3.cloned.1.call-start = ((), (), s32[]{:S(2)}) async-start(), calls=%async_computation | async-start | bytes 7077888 | tf_op jit(solution)/shard_map/psum | solution.py:100
  8.5 41.9 %copy-start.2 = (bf16[27,128,128]{2,1,0:T(8,128)(2,1)S(1)}, bf16[27,128,128]{2,1,0:T(8,128)(2,1)}, u32[]{:S(2)}) copy-start(bf16[27,128,128]{2,1,0:T(8,128)(2,1)} %param.22) | copy-start | bytes 2654212
  10.3 46.7 %collective-permute-start.1 = (bf16[1,8,4,8,128]{4,3,2,1,0:T(8,128)(2,1)}, bf16[1,8,4,8,128]{4,3,2,1,0:T(8,128)(2,1)S(1)}, u32[]{:S(2)}, u32[]{:S(2)}) collective-permute-start(bf16[1,8,4,8,128]{4,3,2,1,0:T(8,128)(2,1)} %get-tuple-element.98), channel_id=1, source_target_pairs={{8,0},{16,8},{24,16},{9,1},{17,9},{25,17},{10,2},{18,10},{26,18},{... | collective-permute-start | bytes 196616 | tf_op jit(solution)/shard_map/ppermute | solution.py:17
  11.6 45.4 %collective-permute-start = (bf16[1,8,4,8,128]{4,3,2,1,0:T(8,128)(2,1)S(1)}, bf16[1,8,4,8,128]{4,3,2,1,0:T(8,128)(2,1)S(1)}, u32[]{:S(2)}, u32[]{:S(2)}) collective-permute-start(bf16[1,8,4,8,128]{4,3,2,1,0:T(8,128)(2,1)S(1)} %get-tuple-element.97), channel_id=1, source_target_pairs={{0,8},{8,16},{16,24},{1,9},{9,17},{17,25},{2,10},{10,18},{18,26},{... | collective-permute-start | bytes 196616 | tf_op jit(solution)/shard_map/ppermute | solution.py:15
  54.0 33.0 %copy-start.51 = (s32[1024]{0:T(1024)}, s32[1024]{0:T(1024)S(1)}, u32[]{:S(2)}) copy-start(s32[1024]{0:T(1024)S(1)} %get-tuple-element.219) | copy-start | bytes 12292
  54.7 32.3 %copy-start.52 = (s32[1024]{0:T(1024)}, s32[1024]{0:T(1024)S(1)}, u32[]{:S(2)}) copy-start(s32[1024]{0:T(1024)S(1)} %get-tuple-element.222) | copy-start | bytes 12292
  54.7 32.3 %copy-start.53 = (s32[1024]{0:T(1024)}, s32[1024]{0:T(1024)S(1)}, u32[]{:S(2)}) copy-start(s32[1024]{0:T(1024)S(1)} %get-tuple-element.221) | copy-start | bytes 12292
  55.4 31.6 %copy-start.48 = (s32[1024]{0:T(1024)}, s32[1024]{0:T(1024)S(1)}, u32[]{:S(2)}) copy-start(s32[1024]{0:T(1024)S(1)} %get-tuple-element.224) | copy-start | bytes 12292
  57.1 13.1 %collective-permute-start.3 = (bf16[10,1,4,8,128]{4,3,2,1,0:T(8,128)(2,1)S(1)}, bf16[10,1,4,8,128]{4,3,2,1,0:T(8,128)(2,1)S(1)}, u32[]{:S(2)}, u32[]{:S(2)}) collective-permute-start(bf16[10,1,4,8,128]{4,3,2,1,0:T(8,128)(2,1)S(1)} %get-tuple-element.82), channel_id=1, source_target_pairs={{2,0},{4,2},{6,4},{3,1},{5,3},{7,5},{10,8},{12,10},{14,12},{11,9},... | collective-permute-start | bytes 245768 | tf_op jit(solution)/shard_map/ppermute | solution.py:17
  58.4 11.9 %collective-permute-start.2 = (bf16[10,1,4,8,128]{4,3,2,1,0:T(8,128)(2,1)S(1)}, bf16[10,1,4,8,128]{4,3,2,1,0:T(8,128)(2,1)S(1)}, u32[]{:S(2)}, u32[]{:S(2)}) collective-permute-start(bf16[10,1,4,8,128]{4,3,2,1,0:T(8,128)(2,1)S(1)} %get-tuple-element.81), channel_id=1, source_target_pairs={{0,2},{2,4},{4,6},{1,3},{3,5},{5,7},{8,10},{10,12},{12,14},{9,11},... | collective-permute-start | bytes 245768 | tf_op jit(solution)/shard_map/ppermute | solution.py:15
  133.3 25.9 %collective-permute-start.5 = (bf16[1,8,4,8,128]{4,3,2,1,0:T(8,128)(2,1)S(1)}, bf16[1,8,4,8,128]{4,3,2,1,0:T(8,128)(2,1)S(1)}, u32[]{:S(2)}, u32[]{:S(2)}) collective-permute-start(bf16[1,8,4,8,128]{4,3,2,1,0:T(8,128)(2,1)S(1)} %get-tuple-element.94), channel_id=1, source_target_pairs={{8,0},{16,8},{24,16},{9,1},{17,9},{25,17},{10,2},{18,10},{26,18},{... | collective-permute-start | bytes 196616 | tf_op jit(solution)/shard_map/ppermute | solution.py:17
  134.6 24.6 %collective-permute-start.4 = (bf16[1,8,4,8,128]{4,3,2,1,0:T(8,128)(2,1)S(1)}, bf16[1,8,4,8,128]{4,3,2,1,0:T(8,128)(2,1)S(1)}, u32[]{:S(2)}, u32[]{:S(2)}) collective-permute-start(bf16[1,8,4,8,128]{4,3,2,1,0:T(8,128)(2,1)S(1)} %get-tuple-element.93), channel_id=1, source_target_pairs={{0,8},{8,16},{16,24},{1,9},{9,17},{17,25},{2,10},{10,18},{18,26},{... | collective-permute-start | bytes 196616 | tf_op jit(solution)/shard_map/ppermute | solution.py:15
  141.1 28.0 %copy-start.23 = (bf16[4]{0:T(256)(128)(2,1)S(1)}, bf16[4]{0:T(256)(128)(2,1)}, u32[]{:S(2)}) copy-start(bf16[4]{0:T(256)(128)(2,1)} %get-tuple-element.52) | copy-start | bytes 28
  141.1 29.6 %copy-start.22 = (bf16[4]{0:T(256)(128)(2,1)S(1)}, bf16[4]{0:T(256)(128)(2,1)}, u32[]{:S(2)}) copy-start(bf16[4]{0:T(256)(128)(2,1)} %get-tuple-element.50) | copy-start | bytes 28
  141.1 29.6 %copy-start.34 = (pred[4]{0:T(512)(128)(4,1)S(1)}, pred[4]{0:T(512)(128)(4,1)}, u32[]{:S(2)}) copy-start(pred[4]{0:T(512)(128)(4,1)} %get-tuple-element.206) | copy-start | bytes 16
  141.1 30.4 %copy-start.13 = (bf16[4]{0:T(256)(128)(2,1)S(1)}, bf16[4]{0:T(256)(128)(2,1)}, u32[]{:S(2)}) copy-start(bf16[4]{0:T(256)(128)(2,1)} %get-tuple-element.28) | copy-start | bytes 28
  141.1 30.4 %copy-start.33 = (pred[4]{0:T(512)(128)(4,1)S(1)}, pred[4]{0:T(512)(128)(4,1)}, u32[]{:S(2)}) copy-start(pred[4]{0:T(512)(128)(4,1)} %get-tuple-element.209) | copy-start | bytes 16
  141.1 32.0 %copy-start.11 = (bf16[4]{0:T(256)(128)(2,1)S(1)}, bf16[4]{0:T(256)(128)(2,1)}, u32[]{:S(2)}) copy-start(bf16[4]{0:T(256)(128)(2,1)} %get-tuple-element.26) | copy-start | bytes 28
  141.2 32.0 %copy-start.30 = (pred[4]{0:T(512)(128)(4,1)S(1)}, pred[4]{0:T(512)(128)(4,1)}, u32[]{:S(2)}) copy-start(pred[4]{0:T(512)(128)(4,1)} %get-tuple-element.211) | copy-start | bytes 16
  141.2 32.9 %copy-start.10 = (bf16[4]{0:T(256)(128)(2,1)S(1)}, bf16[4]{0:T(256)(128)(2,1)}, u32[]{:S(2)}) copy-start(bf16[4]{0:T(256)(128)(2,1)} %get-tuple-element.23) | copy-start | bytes 28
  141.2 32.9 %copy-start.28 = (pred[4]{0:T(512)(128)(4,1)S(1)}, pred[4]{0:T(512)(128)(4,1)}, u32[]{:S(2)}) copy-start(pred[4]{0:T(512)(128)(4,1)} %get-tuple-element.214) | copy-start | bytes 16
  159.3 11.5 %collective-permute-start.7 = (bf16[10,1,4,8,128]{4,3,2,1,0:T(8,128)(2,1)S(1)}, bf16[10,1,4,8,128]{4,3,2,1,0:T(8,128)(2,1)S(1)}, u32[]{:S(2)}, u32[]{:S(2)}) collective-permute-start(bf16[10,1,4,8,128]{4,3,2,1,0:T(8,128)(2,1)S(1)} %get-tuple-element.80), channel_id=1, source_target_pairs={{2,0},{4,2},{6,4},{3,1},{5,3},{7,5},{10,8},{12,10},{14,12},{11,9},... | collective-permute-start | bytes 245768 | tf_op jit(solution)/shard_map/ppermute | solution.py:17
  160.6 12.7 %collective-permute-start.6 = (bf16[10,1,4,8,128]{4,3,2,1,0:T(8,128)(2,1)S(1)}, bf16[10,1,4,8,128]{4,3,2,1,0:T(8,128)(2,1)S(1)}, u32[]{:S(2)}, u32[]{:S(2)}) collective-permute-start(bf16[10,1,4,8,128]{4,3,2,1,0:T(8,128)(2,1)S(1)} %get-tuple-element.79), channel_id=1, source_target_pairs={{0,2},{2,4},{4,6},{1,3},{3,5},{5,7},{8,10},{10,12},{12,14},{9,11},... | collective-permute-start | bytes 245768 | tf_op jit(solution)/shard_map/ppermute | solution.py:15
  230.1 34.9 %collective-permute-start.9 = (bf16[1,8,4,8,128]{4,3,2,1,0:T(8,128)(2,1)S(1)}, bf16[1,8,4,8,128]{4,3,2,1,0:T(8,128)(2,1)S(1)}, u32[]{:S(2)}, u32[]{:S(2)}) collective-permute-start(bf16[1,8,4,8,128]{4,3,2,1,0:T(8,128)(2,1)S(1)} %get-tuple-element.90), channel_id=1, source_target_pairs={{8,0},{16,8},{24,16},{9,1},{17,9},{25,17},{10,2},{18,10},{26,18},{... | collective-permute-start | bytes 196616 | tf_op jit(solution)/shard_map/ppermute | solution.py:17
  231.6 33.4 %collective-permute-start.8 = (bf16[1,8,4,8,128]{4,3,2,1,0:T(8,128)(2,1)S(1)}, bf16[1,8,4,8,128]{4,3,2,1,0:T(8,128)(2,1)S(1)}, u32[]{:S(2)}, u32[]{:S(2)}) collective-permute-start(bf16[1,8,4,8,128]{4,3,2,1,0:T(8,128)(2,1)S(1)} %get-tuple-element.89), channel_id=1, source_target_pairs={{0,8},{8,16},{16,24},{1,9},{9,17},{17,25},{2,10},{10,18},{18,26},{... | collective-permute-start | bytes 196616 | tf_op jit(solution)/shard_map/ppermute | solution.py:15
  265.0 11.6 %collective-permute-start.11 = (bf16[10,1,4,8,128]{4,3,2,1,0:T(8,128)(2,1)S(1)}, bf16[10,1,4,8,128]{4,3,2,1,0:T(8,128)(2,1)S(1)}, u32[]{:S(2)}, u32[]{:S(2)}) collective-permute-start(bf16[10,1,4,8,128]{4,3,2,1,0:T(8,128)(2,1)S(1)} %get-tuple-element.78), channel_id=1, source_target_pairs={{2,0},{4,2},{6,4},{3,1},{5,3},{7,5},{10,8},{12,10},{14,12},{11,9},... | collective-permute-start | bytes 245768 | tf_op jit(solution)/shard_map/ppermute | solution.py:17
  266.3 12.7 %collective-permute-start.10 = (bf16[10,1,4,8,128]{4,3,2,1,0:T(8,128)(2,1)S(1)}, bf16[10,1,4,8,128]{4,3,2,1,0:T(8,128)(2,1)S(1)}, u32[]{:S(2)}, u32[]{:S(2)}) collective-permute-start(bf16[10,1,4,8,128]{4,3,2,1,0:T(8,128)(2,1)S(1)} %get-tuple-element.77), channel_id=1, source_target_pairs={{0,2},{2,4},{4,6},{1,3},{3,5},{5,7},{8,10},{10,12},{12,14},{9,11},... | collective-permute-start | bytes 245768 | tf_op jit(solution)/shard_map/ppermute | solution.py:15
  334.3 16.2 %collective-permute-start.13 = (bf16[1,8,4,8,128]{4,3,2,1,0:T(8,128)(2,1)S(1)}, bf16[1,8,4,8,128]{4,3,2,1,0:T(8,128)(2,1)S(1)}, u32[]{:S(2)}, u32[]{:S(2)}) collective-permute-start(bf16[1,8,4,8,128]{4,3,2,1,0:T(8,128)(2,1)S(1)} %get-tuple-element.86), channel_id=1, source_target_pairs={{8,0},{16,8},{24,16},{9,1},{17,9},{25,17},{10,2},{18,10},{26,18},{... | collective-permute-start | bytes 196616 | tf_op jit(solution)/shard_map/ppermute | solution.py:17
  335.6 14.9 %collective-permute-start.12 = (bf16[1,8,4,8,128]{4,3,2,1,0:T(8,128)(2,1)S(1)}, bf16[1,8,4,8,128]{4,3,2,1,0:T(8,128)(2,1)S(1)}, u32[]{:S(2)}, u32[]{:S(2)}) collective-permute-start(bf16[1,8,4,8,128]{4,3,2,1,0:T(8,128)(2,1)S(1)} %get-tuple-element.85), channel_id=1, source_target_pairs={{0,8},{8,16},{16,24},{1,9},{9,17},{17,25},{2,10},{10,18},{18,26},{... | collective-permute-start | bytes 196616 | tf_op jit(solution)/shard_map/ppermute | solution.py:15
  350.5 11.6 %collective-permute-start.15 = (bf16[10,1,4,8,128]{4,3,2,1,0:T(8,128)(2,1)S(1)}, bf16[10,1,4,8,128]{4,3,2,1,0:T(8,128)(2,1)S(1)}, u32[]{:S(2)}, u32[]{:S(2)}) collective-permute-start(bf16[10,1,4,8,128]{4,3,2,1,0:T(8,128)(2,1)S(1)} %get-tuple-element.76), channel_id=1, source_target_pairs={{2,0},{4,2},{6,4},{3,1},{5,3},{7,5},{10,8},{12,10},{14,12},{11,9},... | collective-permute-start | bytes 245768 | tf_op jit(solution)/shard_map/ppermute | solution.py:17
  351.8 12.7 %collective-permute-start.14 = (bf16[10,1,4,8,128]{4,3,2,1,0:T(8,128)(2,1)S(1)}, bf16[10,1,4,8,128]{4,3,2,1,0:T(8,128)(2,1)S(1)}, u32[]{:S(2)}, u32[]{:S(2)}) collective-permute-start(bf16[10,1,4,8,128]{4,3,2,1,0:T(8,128)(2,1)S(1)} %get-tuple-element.75), channel_id=1, source_target_pairs={{0,2},{2,4},{4,6},{1,3},{3,5},{5,7},{8,10},{10,12},{12,14},{9,11},... | collective-permute-start | bytes 245768 | tf_op jit(solution)/shard_map/ppermute | solution.py:15
  (47 other events, 678.7 us)
Sparse Core Ops, SparseCore 0:
  350.6 140.2 all-reduce.2
where the time goes:
time: 508 us; the launch traced here: 502 us
  local copies, waits for them, and re-layouts  213 us (42%)
  other arithmetic  96.7 us (19%)
  waiting for transfers between devices  72.4 us (14%)
  matrix products  52.4 us (10%)
  starting transfers between devices  51 us (10%)
  between operations  17.3 us (3%)
    unnamed x253, local copies, waits for them, and re-layouts  97.8 us
    psum x1, waiting for transfers between devices, sum_gradients(): lax.psum((first_part, second_part), ('sx', 'sy', 'dp'))  72.3 us
    gather x104, local copies, waits for them, and re-layouts, padded_blocks(): slab_piece = jnp.take(region, jnp.maximum(target, 0), axis=2) * valid  70.7 us
    ppermute x8, starting transfers between devices, with_halo(): lax.ppermute(tail, axis, [(i, (i + 1) % count) for i in range(ends)])  40.4 us
    dot_general x2, local copies, waits for them, and re-layouts, weight_partial(): lax.dot_general(columns, grads.reshape(-1, channels), (((0,), (0,)), ((),...  36.7 us
    dot_general x4, matrix products, convolve(): jnp.dot(columns, matrix, preferred_element_type=jnp.float32).reshape(shape)  35.9 us
    concatenate x8, other arithmetic, padded_blocks(): return jnp.concatenate(planes, axis=0)  21.7 us
    mul x104, other arithmetic, padded_blocks(): slab_piece = jnp.take(region, jnp.maximum(target, 0), axis=2) * valid  18.3 us
  transfers between devices with their start and end apart: 17, of which 1 were waited for; matrix products, arithmetic and copies ran while one was open for 36% of the time, Pallas kernels for 0%

commit v1 on v0

--- a/solution.py
+++ b/solution.py
@@ -97,7 +97,7 @@
 
 
 def sum_gradients(first_part, second_part):
-    first_total, second_total = lax.psum((first_part, second_part), ("sx", "sy", "dp"))
+    first_total, second_total = lax.psum(lax.psum((first_part, second_part), ("sy", "dp")), "sx")
     return (first_total, second_total)
 
 

time: 508 us -> 573 us (1.13)
  waiting for transfers between devices: 72.4 us -> 128 us
  other arithmetic: 96.7 us -> 108 us
    psum x1 -> x2, waiting for transfers between devices: 72.3 us -> 128 us  [the longest x1 117 us: sum_gradients(): lax.psum(lax.psum((first_part, second_part), ('sy', 'dp')), 'sx')]
    mul x104, other arithmetic: 18.3 us -> 27.7 us  [padded_blocks(): slab_piece = jnp.take(region, jnp.maximum(target, 0), axis=2) * valid]
    unnamed x253 -> x323, local copies, waits for them, and re-layouts: 97.8 us -> 91.5 us
  transfers between devices with their start and end apart: 17 -> 18, of which waited for: 1 -> 2; matrix products, arithmetic and copies ran while one was open for 36% -> 35% of each run, Pallas kernels for 0% -> 0%
where the time goes in v1:
time: 573 us; the launch traced here: 567 us
  local copies, waits for them, and re-layouts  210 us (37%)
  waiting for transfers between devices  128 us (22%)
  other arithmetic  108 us (19%)
  matrix products  52.4 us (9%)
  starting transfers between devices  50.8 us (9%)
  between operations  17.8 us (3%)
    psum x1, waiting for transfers between devices, sum_gradients(): lax.psum(lax.psum((first_part, second_part), ('sy', 'dp')), 'sx')  117 us
    unnamed x323, local copies, waits for them, and re-layouts  91.5 us
    gather x104, local copies, waits for them, and re-layouts, padded_blocks(): slab_piece = jnp.take(region, jnp.maximum(target, 0), axis=2) * valid  70.9 us
    ppermute x8, starting transfers between devices, with_halo(): lax.ppermute(tail, axis, [(i, (i + 1) % count) for i in range(ends)])  40.4 us
    dot_general x2, local copies, waits for them, and re-layouts, weight_partial(): lax.dot_general(columns, grads.reshape(-1, channels), (((0,), (0,)), ((),...  37.4 us
    dot_general x4, matrix products, convolve(): jnp.dot(columns, matrix, preferred_element_type=jnp.float32).reshape(shape)  35.9 us
    mul x104, other arithmetic, padded_blocks(): slab_piece = jnp.take(region, jnp.maximum(target, 0), axis=2) * valid  27.7 us
    concatenate x8, other arithmetic, padded_blocks(): return jnp.concatenate(planes, axis=0)  23 us
  transfers between devices with their start and end apart: 18, of which 2 were waited for; matrix products, arithmetic and copies ran while one was open for 35% of the time, Pallas kernels for 0%

profile of v1, /device:TPU:0, one launch (start us, length us, event | category | flops | bytes accessed | tf_op | source)
XLA Modules:
  0.0 566.8 jit_solution(13415092686359116927)
XLA Ops:
  11.6 5.6 collective-permute-start
  19.1 2.5 fusion.137
  59.1 4.7 collective-permute-start.2
  88.5 2.2 maximum_maximum_fusion
  113.7 3.2 maximum_maximum_fusion.1
  126.1 8.5 %multiply_convert_fusion.1 = (bf16[8,8,4,8,128]{4,3,2,1,0:T(8,128)(2,1)S(1)}, f32[8,8,4,8,128]{4,3,2,1,0:T(8,128)}) fusion(f32[4]{0:T(128)S(1)} %copy-done.91, bf16[8,8,4,8,3456]{4,3,2,1,0:T(8,128)(2,1)} %slice_dynamic-update-slice_fusion.72, bf16[3456,128,1,1,1]{1,0,4,3,2:T(8,128)(2,1)S(1)} %bitcast.657), kind=kOutput, calls=%fused_computation.133 | convolution fusion | flops 1813512192 | bytes 16613392 | tf_op jit(solution)/shard_map/dot_general | solution.py:85
  136.1 4.5 collective-permute-start.4
  142.7 18.7 %copy.150 = bf16[3456,2048]{1,0:T(8,128)(2,1)} copy(bf16[3456,2048]{0,1:T(8,128)(2,1)} %bitcast.253) | data formatting | bytes 28311552 | tf_op jit(solution)/shard_map/dot_general | solution.py:90
  162.9 5.4 collective-permute-start.6
  182.8 2.0 maximum_maximum_fusion.11
  184.8 2.2 maximum_maximum_fusion.2
  209.6 3.2 maximum_maximum_fusion.3
  222.0 10.1 %fusion.6 = (bf16[8,8,4,8,128]{4,3,2,1,0:T(8,128)(2,1)S(1)}, bf16[1,8,8,4,8,128]{5,4,3,2,1,0:T(8,128)(2,1)}) fusion(bf16[1,8,8,4,8,128]{5,4,3,2,1,0:T(8,128)(2,1)S(1)} %copy-done.95, f32[4]{0:T(128)S(1)} %copy-done.91, bf16[8,8,4,8,3456]{4,3,2,1,0:T(8,128)(2,1)} %slice_dynamic-update-slice_fusion.48, bf16[3456,128,1,1,1]{1,0,4,3,2:T(8,128)(2,1)S(1)} %bitcast.658, ...), kind=kOutput, calls=%fused_computation.130 | convolution fusion | flops 1816133632 | bytes 17137680 | tf_op jit(solution)/shard_map/dot_general | solution.py:85
  233.6 4.7 collective-permute-start.8
  240.0 18.7 %copy.151 = bf16[3456,2048]{1,0:T(8,128)(2,1)} copy(bf16[3456,2048]{0,1:T(8,128)(2,1)} %bitcast.258) | data formatting | bytes 28311552 | tf_op jit(solution)/shard_map/dot_general | solution.py:90
  258.7 8.3 %fusion.180 = f32[27,128,128]{2,1,0:T(8,128)} fusion(bf16[27,128,2048]{2,1,0:T(8,128)(2,1)} %bitcast.651, bf16[2048,128,1]{1,0,2:T(8,128)(2,1)S(1)} %bitcast.648), kind=kOutput, calls=%fused_computation.762 | convolution fusion | flops 1811939328 | bytes 16449536 | tf_op jit(solution)/shard_map/dot_general | solution.py:90
  268.5 5.5 collective-permute-start.10
  289.9 2.2 maximum_maximum_fusion.4
  296.2 5.0 copy-done.20
  305.9 3.5 maximum_maximum_fusion.5
  318.5 9.1 %fusion.3 = bf16[8,8,4,8,128]{4,3,2,1,0:T(8,128)(2,1)S(1)} fusion(bf16[8,8,4,8,3456]{4,3,2,1,0:T(8,128)(2,1)} %slice_dynamic-update-slice_fusion.24, bf16[3456,128,1,1,1]{1,0,4,3,2:T(8,128)(2,1)S(1)} %bitcast.659, f32[8,8,4,8,128]{4,3,2,1,0:T(8,128)S(1)} %copy-done.96, f32[4]{0:T(128)S(1)} %copy-done.91), kind=kOutput, calls=%fused_computation.118 | convolution fusion | flops 1814560768 | bytes 16613392 | tf_op jit(solution)/shard_map/dot_general | solution.py:85
  329.1 4.5 collective-permute-start.12
  335.3 8.3 %fusion.179 = f32[27,128,128]{2,1,0:T(8,128)} fusion(bf16[27,128,2048]{2,1,0:T(8,128)(2,1)} %bitcast.650, bf16[2048,128,1]{1,0,2:T(8,128)(2,1)S(1)} %bitcast.649), kind=kOutput, calls=%fused_computation.761 | convolution fusion | flops 1811939328 | bytes 16449536 | tf_op jit(solution)/shard_map/dot_general | solution.py:90
  345.2 5.4 collective-permute-start.14
  374.6 2.5 maximum_maximum_fusion.15
  377.2 2.2 maximum_maximum_fusion.6
  403.1 4.3 maximum_maximum_fusion.7
  407.4 11.5 %all-reduce.5.cloned.1.call-done = (f32[27,128,128]{2,1,0:T(8,128)}, f32[27,128,128]{2,1,0:T(8,128)}) async-done(((f32[27,128,128]{2,1,0:T(8,128)}, f32[27,128,128]{2,1,0:T(8,128)}), (f32[27,128,128]{2,1,0:T(8,128)}, f32[27,128,128]{2,1,0:T(8,128)})) %all-reduce.5.cloned.1.call-update) | async-done | bytes 3538960 | tf_op jit(solution)/shard_map/psum | solution.py:100
  419.0 2.3 slice_dynamic-update-slice_fusion.9
  430.4 8.2 %fusion.4 = bf16[1,8,8,4,8,128]{5,4,3,2,1,0:T(8,128)(2,1)} fusion(bf16[8,8,4,8,3456]{4,3,2,1,0:T(8,128)(2,1)} %slice_dynamic-update-slice_fusion, bf16[3456,128,1,1,1]{1,0,4,3,2:T(8,128)(2,1)S(1)} %bitcast.656, bf16[8,8,4,8,128]{4,3,2,1,0:T(8,128)(2,1)S(1)} %get-tuple-element.67, f32[4]{0:T(128)S(1)} %copy-done.92), kind=kOutput, calls=%fused_computation.119 | convolution fusion | flops 1812987904 | bytes 16089104 | tf_op jit(solution)/shard_map/dot_general | solution.py:85
  438.6 116.7 %all-reduce.7.cloned.1.call-done = (f32[27,128,128]{2,1,0:T(8,128)}, f32[27,128,128]{2,1,0:T(8,128)}) async-done(((f32[27,128,128]{2,1,0:T(8,128)}, f32[27,128,128]{2,1,0:T(8,128)}), (f32[27,128,128]{2,1,0:T(8,128)}, f32[27,128,128]{2,1,0:T(8,128)})) %all-reduce.7.cloned.1.call-update) | async-done | bytes 3538960 | tf_op jit(solution)/shard_map/psum | solution.py:100
  555.3 3.0 broadcast_multiply_fusion.1
  (726 shorter events, 250.4 us)
Async XLA Ops:
  7.2 40.6 %copy-start.7 = (bf16[27,128,128]{2,1,0:T(8,128)(2,1)S(1)}, bf16[27,128,128]{2,1,0:T(8,128)(2,1)}, u32[]{:S(2)}) copy-start(bf16[27,128,128]{2,1,0:T(8,128)(2,1)} %param.23) | copy-start | bytes 2654212
  7.2 411.8 %all-reduce.5.cloned.1.call-start = ((), (), s32[]{:S(2)}) async-start(), calls=%async_computation | async-start | bytes 7077888 | tf_op jit(solution)/shard_map/psum | solution.py:100
  8.4 41.7 %copy-start.6 = (bf16[27,128,128]{2,1,0:T(8,128)(2,1)S(1)}, bf16[27,128,128]{2,1,0:T(8,128)(2,1)}, u32[]{:S(2)}) copy-start(bf16[27,128,128]{2,1,0:T(8,128)(2,1)} %param.22) | copy-start | bytes 2654212
  10.3 47.4 %collective-permute-start.1 = (bf16[1,8,4,8,128]{4,3,2,1,0:T(8,128)(2,1)}, bf16[1,8,4,8,128]{4,3,2,1,0:T(8,128)(2,1)S(1)}, u32[]{:S(2)}, u32[]{:S(2)}) collective-permute-start(bf16[1,8,4,8,128]{4,3,2,1,0:T(8,128)(2,1)} %get-tuple-element.100), channel_id=1, source_target_pairs={{8,0},{16,8},{24,16},{9,1},{17,9},{25,17},{10,2},{18,10},{26,18},{... | collective-permute-start | bytes 196616 | tf_op jit(solution)/shard_map/ppermute | solution.py:17
  11.6 46.1 %collective-permute-start = (bf16[1,8,4,8,128]{4,3,2,1,0:T(8,128)(2,1)S(1)}, bf16[1,8,4,8,128]{4,3,2,1,0:T(8,128)(2,1)S(1)}, u32[]{:S(2)}, u32[]{:S(2)}) collective-permute-start(bf16[1,8,4,8,128]{4,3,2,1,0:T(8,128)(2,1)S(1)} %get-tuple-element.99), channel_id=1, source_target_pairs={{0,8},{8,16},{16,24},{1,9},{9,17},{17,25},{2,10},{10,18},{18,26},{... | collective-permute-start | bytes 196616 | tf_op jit(solution)/shard_map/ppermute | solution.py:15
  21.6 261.2 %copy-start.21 = (bf16[4]{0:T(256)(128)(2,1)}, bf16[4]{0:T(256)(128)(2,1)S(1)}, u32[]{:S(2)}) copy-start(bf16[4]{0:T(256)(128)(2,1)S(1)} %get-tuple-element.22) | copy-start | bytes 28
  22.4 260.4 %copy-start.23 = (pred[4]{0:T(512)(128)(4,1)}, pred[4]{0:T(512)(128)(4,1)S(1)}, u32[]{:S(2)}) copy-start(pred[4]{0:T(512)(128)(4,1)S(1)} %get-tuple-element.217) | copy-start | bytes 16
  34.2 246.1 %copy-start.25 = (pred[4]{0:T(512)(128)(4,1)}, pred[4]{0:T(512)(128)(4,1)S(1)}, u32[]{:S(2)}) copy-start(pred[4]{0:T(512)(128)(4,1)S(1)} %get-tuple-element.212) | copy-start | bytes 16
  57.8 13.0 %collective-permute-start.3 = (bf16[10,1,4,8,128]{4,3,2,1,0:T(8,128)(2,1)S(1)}, bf16[10,1,4,8,128]{4,3,2,1,0:T(8,128)(2,1)S(1)}, u32[]{:S(2)}, u32[]{:S(2)}) collective-permute-start(bf16[10,1,4,8,128]{4,3,2,1,0:T(8,128)(2,1)S(1)} %get-tuple-element.84), channel_id=1, source_target_pairs={{2,0},{4,2},{6,4},{3,1},{5,3},{7,5},{10,8},{12,10},{14,12},{11,9},... | collective-permute-start | bytes 245768 | tf_op jit(solution)/shard_map/ppermute | solution.py:17
  59.1 11.8 %collective-permute-start.2 = (bf16[10,1,4,8,128]{4,3,2,1,0:T(8,128)(2,1)S(1)}, bf16[10,1,4,8,128]{4,3,2,1,0:T(8,128)(2,1)S(1)}, u32[]{:S(2)}, u32[]{:S(2)}) collective-permute-start(bf16[10,1,4,8,128]{4,3,2,1,0:T(8,128)(2,1)S(1)} %get-tuple-element.83), channel_id=1, source_target_pairs={{0,2},{2,4},{4,6},{1,3},{3,5},{5,7},{8,10},{10,12},{12,14},{9,11},... | collective-permute-start | bytes 245768 | tf_op jit(solution)/shard_map/ppermute | solution.py:15
  134.8 26.7 %collective-permute-start.5 = (bf16[1,8,4,8,128]{4,3,2,1,0:T(8,128)(2,1)S(1)}, bf16[1,8,4,8,128]{4,3,2,1,0:T(8,128)(2,1)S(1)}, u32[]{:S(2)}, u32[]{:S(2)}) collective-permute-start(bf16[1,8,4,8,128]{4,3,2,1,0:T(8,128)(2,1)S(1)} %get-tuple-element.96), channel_id=1, source_target_pairs={{8,0},{16,8},{24,16},{9,1},{17,9},{25,17},{10,2},{18,10},{26,18},{... | collective-permute-start | bytes 196616 | tf_op jit(solution)/shard_map/ppermute | solution.py:17
  136.1 25.4 %collective-permute-start.4 = (bf16[1,8,4,8,128]{4,3,2,1,0:T(8,128)(2,1)S(1)}, bf16[1,8,4,8,128]{4,3,2,1,0:T(8,128)(2,1)S(1)}, u32[]{:S(2)}, u32[]{:S(2)}) collective-permute-start(bf16[1,8,4,8,128]{4,3,2,1,0:T(8,128)(2,1)S(1)} %get-tuple-element.95), channel_id=1, source_target_pairs={{0,8},{8,16},{16,24},{1,9},{9,17},{17,25},{2,10},{10,18},{18,26},{... | collective-permute-start | bytes 196616 | tf_op jit(solution)/shard_map/ppermute | solution.py:15
  142.6 30.4 %copy-start.47 = (bf16[4]{0:T(256)(128)(2,1)S(1)}, bf16[4]{0:T(256)(128)(2,1)}, u32[]{:S(2)}) copy-start(bf16[4]{0:T(256)(128)(2,1)} %get-tuple-element.50) | copy-start | bytes 28
  142.6 30.4 %copy-start.60 = (pred[4]{0:T(512)(128)(4,1)S(1)}, pred[4]{0:T(512)(128)(4,1)}, u32[]{:S(2)}) copy-start(pred[4]{0:T(512)(128)(4,1)} %get-tuple-element.208) | copy-start | bytes 16
  142.6 31.2 %copy-start.36 = (bf16[4]{0:T(256)(128)(2,1)S(1)}, bf16[4]{0:T(256)(128)(2,1)}, u32[]{:S(2)}) copy-start(bf16[4]{0:T(256)(128)(2,1)} %get-tuple-element.28) | copy-start | bytes 28
  142.6 31.2 %copy-start.59 = (pred[4]{0:T(512)(128)(4,1)S(1)}, pred[4]{0:T(512)(128)(4,1)}, u32[]{:S(2)}) copy-start(pred[4]{0:T(512)(128)(4,1)} %get-tuple-element.211) | copy-start | bytes 16
  142.6 32.8 %copy-start.34 = (bf16[4]{0:T(256)(128)(2,1)S(1)}, bf16[4]{0:T(256)(128)(2,1)}, u32[]{:S(2)}) copy-start(bf16[4]{0:T(256)(128)(2,1)} %get-tuple-element.26) | copy-start | bytes 28
  142.7 32.8 %copy-start.57 = (pred[4]{0:T(512)(128)(4,1)S(1)}, pred[4]{0:T(512)(128)(4,1)}, u32[]{:S(2)}) copy-start(pred[4]{0:T(512)(128)(4,1)} %get-tuple-element.213) | copy-start | bytes 16
  142.7 33.6 %copy-start.32 = (bf16[4]{0:T(256)(128)(2,1)S(1)}, bf16[4]{0:T(256)(128)(2,1)}, u32[]{:S(2)}) copy-start(bf16[4]{0:T(256)(128)(2,1)} %get-tuple-element.23) | copy-start | bytes 28
  142.7 33.6 %copy-start.55 = (pred[4]{0:T(512)(128)(4,1)S(1)}, pred[4]{0:T(512)(128)(4,1)}, u32[]{:S(2)}) copy-start(pred[4]{0:T(512)(128)(4,1)} %get-tuple-element.216) | copy-start | bytes 16
  161.6 11.5 %collective-permute-start.7 = (bf16[10,1,4,8,128]{4,3,2,1,0:T(8,128)(2,1)S(1)}, bf16[10,1,4,8,128]{4,3,2,1,0:T(8,128)(2,1)S(1)}, u32[]{:S(2)}, u32[]{:S(2)}) collective-permute-start(bf16[10,1,4,8,128]{4,3,2,1,0:T(8,128)(2,1)S(1)} %get-tuple-element.82), channel_id=1, source_target_pairs={{2,0},{4,2},{6,4},{3,1},{5,3},{7,5},{10,8},{12,10},{14,12},{11,9},... | collective-permute-start | bytes 245768 | tf_op jit(solution)/shard_map/ppermute | solution.py:17
  162.9 12.7 %collective-permute-start.6 = (bf16[10,1,4,8,128]{4,3,2,1,0:T(8,128)(2,1)S(1)}, bf16[10,1,4,8,128]{4,3,2,1,0:T(8,128)(2,1)S(1)}, u32[]{:S(2)}, u32[]{:S(2)}) collective-permute-start(bf16[10,1,4,8,128]{4,3,2,1,0:T(8,128)(2,1)S(1)} %get-tuple-element.81), channel_id=1, source_target_pairs={{0,2},{2,4},{4,6},{1,3},{3,5},{5,7},{8,10},{10,12},{12,14},{9,11},... | collective-permute-start | bytes 245768 | tf_op jit(solution)/shard_map/ppermute | solution.py:15
  232.3 34.8 %collective-permute-start.9 = (bf16[1,8,4,8,128]{4,3,2,1,0:T(8,128)(2,1)S(1)}, bf16[1,8,4,8,128]{4,3,2,1,0:T(8,128)(2,1)S(1)}, u32[]{:S(2)}, u32[]{:S(2)}) collective-permute-start(bf16[1,8,4,8,128]{4,3,2,1,0:T(8,128)(2,1)S(1)} %get-tuple-element.92), channel_id=1, source_target_pairs={{8,0},{16,8},{24,16},{9,1},{17,9},{25,17},{10,2},{18,10},{26,18},{... | collective-permute-start | bytes 196616 | tf_op jit(solution)/shard_map/ppermute | solution.py:17
  233.6 33.5 %collective-permute-start.8 = (bf16[1,8,4,8,128]{4,3,2,1,0:T(8,128)(2,1)S(1)}, bf16[1,8,4,8,128]{4,3,2,1,0:T(8,128)(2,1)S(1)}, u32[]{:S(2)}, u32[]{:S(2)}) collective-permute-start(bf16[1,8,4,8,128]{4,3,2,1,0:T(8,128)(2,1)S(1)} %get-tuple-element.91), channel_id=1, source_target_pairs={{0,8},{8,16},{16,24},{1,9},{9,17},{17,25},{2,10},{10,18},{18,26},{... | collective-permute-start | bytes 196616 | tf_op jit(solution)/shard_map/ppermute | solution.py:15
  267.2 11.6 %collective-permute-start.11 = (bf16[10,1,4,8,128]{4,3,2,1,0:T(8,128)(2,1)S(1)}, bf16[10,1,4,8,128]{4,3,2,1,0:T(8,128)(2,1)S(1)}, u32[]{:S(2)}, u32[]{:S(2)}) collective-permute-start(bf16[10,1,4,8,128]{4,3,2,1,0:T(8,128)(2,1)S(1)} %get-tuple-element.80), channel_id=1, source_target_pairs={{2,0},{4,2},{6,4},{3,1},{5,3},{7,5},{10,8},{12,10},{14,12},{11,9},... | collective-permute-start | bytes 245768 | tf_op jit(solution)/shard_map/ppermute | solution.py:17
  268.5 12.7 %collective-permute-start.10 = (bf16[10,1,4,8,128]{4,3,2,1,0:T(8,128)(2,1)S(1)}, bf16[10,1,4,8,128]{4,3,2,1,0:T(8,128)(2,1)S(1)}, u32[]{:S(2)}, u32[]{:S(2)}) collective-permute-start(bf16[10,1,4,8,128]{4,3,2,1,0:T(8,128)(2,1)S(1)} %get-tuple-element.79), channel_id=1, source_target_pairs={{0,2},{2,4},{4,6},{1,3},{3,5},{5,7},{8,10},{10,12},{12,14},{9,11},... | collective-permute-start | bytes 245768 | tf_op jit(solution)/shard_map/ppermute | solution.py:15
  327.8 16.1 %collective-permute-start.13 = (bf16[1,8,4,8,128]{4,3,2,1,0:T(8,128)(2,1)S(1)}, bf16[1,8,4,8,128]{4,3,2,1,0:T(8,128)(2,1)S(1)}, u32[]{:S(2)}, u32[]{:S(2)}) collective-permute-start(bf16[1,8,4,8,128]{4,3,2,1,0:T(8,128)(2,1)S(1)} %get-tuple-element.88), channel_id=1, source_target_pairs={{8,0},{16,8},{24,16},{9,1},{17,9},{25,17},{10,2},{18,10},{26,18},{... | collective-permute-start | bytes 196616 | tf_op jit(solution)/shard_map/ppermute | solution.py:17
  329.1 14.8 %collective-permute-start.12 = (bf16[1,8,4,8,128]{4,3,2,1,0:T(8,128)(2,1)S(1)}, bf16[1,8,4,8,128]{4,3,2,1,0:T(8,128)(2,1)S(1)}, u32[]{:S(2)}, u32[]{:S(2)}) collective-permute-start(bf16[1,8,4,8,128]{4,3,2,1,0:T(8,128)(2,1)S(1)} %get-tuple-element.87), channel_id=1, source_target_pairs={{0,8},{8,16},{16,24},{1,9},{9,17},{17,25},{2,10},{10,18},{18,26},{... | collective-permute-start | bytes 196616 | tf_op jit(solution)/shard_map/ppermute | solution.py:15
  343.8 47.7 %copy-start.1 = (bf16[8,8,4,1,128]{4,3,2,1,0:T(2,128)(2,1)}, bf16[8,8,4,1,128]{4,3,2,1,0:T(2,128)(2,1)S(1)}, u32[]{:S(2)}) copy-start(bf16[8,8,4,1,128]{4,3,2,1,0:T(2,128)(2,1)S(1)} %fusion.17) | copy-start | bytes 196612
  343.8 211.5 %all-reduce.7.cloned.1.call-start = ((), (), s32[]{:S(2)}) async-start(), calls=%async_computation.1 | async-start | bytes 7077888 | tf_op jit(solution)/shard_map/psum | solution.py:100
  343.9 15.1 %collective-permute-start.15 = (bf16[10,1,4,8,128]{4,3,2,1,0:T(8,128)(2,1)S(1)}, bf16[10,1,4,8,128]{4,3,2,1,0:T(8,128)(2,1)S(1)}, u32[]{:S(2)}, u32[]{:S(2)}) collective-permute-start(bf16[10,1,4,8,128]{4,3,2,1,0:T(8,128)(2,1)S(1)} %get-tuple-element.78), channel_id=1, source_target_pairs={{2,0},{4,2},{6,4},{3,1},{5,3},{7,5},{10,8},{12,10},{14,12},{11,9},... | collective-permute-start | bytes 245768 | tf_op jit(solution)/shard_map/ppermute | solution.py:17
  345.2 16.3 %collective-permute-start.14 = (bf16[10,1,4,8,128]{4,3,2,1,0:T(8,128)(2,1)S(1)}, bf16[10,1,4,8,128]{4,3,2,1,0:T(8,128)(2,1)S(1)}, u32[]{:S(2)}, u32[]{:S(2)}) collective-permute-start(bf16[10,1,4,8,128]{4,3,2,1,0:T(8,128)(2,1)S(1)} %get-tuple-element.77), channel_id=1, source_target_pairs={{0,2},{2,4},{4,6},{1,3},{3,5},{5,7},{8,10},{10,12},{12,14},{9,11},... | collective-permute-start | bytes 245768 | tf_op jit(solution)/shard_map/ppermute | solution.py:15
  (83 other events, 1046.3 us)
Sparse Core Ops, SparseCore 0:
  343.9 74.9 all-reduce.4
  421.4 133.8 all-reduce.6
